TPU v7x, 512 devices: a whole 4x4x16 slice. The times are simulated.
512 devices in a mesh: site: 64 (over y, z), vec: 8 (over x, core).
Axes of the slice: x: 4, y: 4, z: 16, core: 2. Of those that a mesh axis runs over, the one named last changes fastest.
Arguments:
- diag_blocks: float32 [512, 64, 128], P('site'), as said below
- hop_blocks: float32 [512, 4, 64, 128], P('site'), may hold values from -0.1875 to 0.1875
- neighbors: int32 [512, 8], P('site'), may hold values from 0 to 511, as said below
- start_basis: float32 [512, 128, 512], P('site', None, 'vec'), may hold values from -6 to 6
Outputs:
- basis: float32 [512, 128, 512], P('site', None, 'vec')
- projected: float32 [512, 512], P(None, 'vec')
Inputs may be any that keep to these rules, and one draw needn't show every extreme that they name: neighbors[s, d] is the site one step forward (d = 0, 1, 2, 3 along x, y, z, t) or back (d = 4 + k along the same k) of site s on a periodic 2 x 2 x 2 x 64 lattice; rows j * 8 to (j + 1) * 8 - 1 hold time slice j in an arbitrary order, so the t neighbours lie in the next and previous slice (wrapping) and the others in the same slice. `diag_blocks`: each diagonal block is Hermitian: its left half is symmetric and its right half antisymmetric.
All inputs are finite; a program needn't handle non-finite values.
Results may differ from a plain program's by a relative error of at most 0.00021.
Values sent between devices are 32-bit elements; how exact they have to be, the bound alone decides.
No kernel may reach another device: no remote copies, remote signals or barrier semaphores. Data moves between devices by JAX's collectives and lax.ppermute only.
A program may use at most 64 MiB of HBM per device.

v0:
```python
import jax
import jax.numpy as jnp
from jax import lax
from jax.sharding import PartitionSpec as P

DEGREE = 4
filter_center = 3.7
filter_radius = 3.1
highest = lax.Precision.HIGHEST


def passed_along(x, axis, by):
    size = lax.axis_size(axis)
    return lax.ppermute(x, axis, [(i, (i + by) % size) for i in range(size)])


def embed(weights):
    half_size = weights.shape[-2]
    real_part = weights[..., :half_size]
    imag_part = weights[..., half_size:]
    upper_rows = jnp.concatenate([real_part, -imag_part], -1)
    lower_rows = jnp.concatenate([imag_part, real_part], -1)
    return jnp.concatenate([upper_rows, lower_rows], -2)


def operate(vectors, matrices, pool_index, time_back):
    ahead_block = passed_along(vectors, "site", -1)
    pool = jnp.concatenate([vectors, ahead_block], 0)
    sources = jnp.take(pool, pool_index[:, :8], axis=0)
    summed = jnp.einsum("sjab,sjbc->sac", matrices, sources, precision=highest)
    backward = jnp.einsum("sba,sbc->sac", time_back, vectors, precision=highest)
    backward = passed_along(backward, "site", 1)
    return summed + jnp.take(backward, pool_index[:, 8], axis=0)


def filtered(start_block, operator_apply):
    previous = start_block
    current = (operator_apply(start_block) - filter_center * start_block) / filter_radius
    for order_step in range(DEGREE - 1):
        following = (
            2.0 * (operator_apply(current) - filter_center * current) / filter_radius - previous
        )
        previous, current = (current, following)
    return current


def factor_inverse(gram_matrix):
    lower_factor = jnp.linalg.cholesky(gram_matrix)
    identity = jnp.eye(gram_matrix.shape[0], dtype=jnp.float32)
    return jax.scipy.linalg.solve_triangular(lower_factor, identity, lower=True)


def local(diag_blocks, hop_blocks, neighbors, start_basis):
    site_count = start_basis.shape[0]
    local_cols = start_basis.shape[2]
    all_cols = local_cols * lax.axis_size("vec")
    total_rows = site_count * start_basis.shape[1] * lax.axis_size("site")
    col_start = lax.axis_index("vec") * local_cols
    row_index = neighbors % site_count
    own_index = jnp.arange(site_count, dtype=jnp.int32)
    diag_full = embed(diag_blocks)
    hop_full = embed(hop_blocks)
    back_list = []
    for direction in range(3):
        chosen = jnp.take(hop_full[:, direction], row_index[:, 4 + direction], axis=0)
        back_list.append(jnp.swapaxes(chosen, 1, 2))
    matrices = jnp.stack(
        [diag_full, hop_full[:, 0], hop_full[:, 1], hop_full[:, 2], hop_full[:, 3]] + back_list, 1
    )
    pool_index = jnp.stack(
        [
            own_index,
            row_index[:, 0],
            row_index[:, 1],
            row_index[:, 2],
            row_index[:, 3] + site_count,
            row_index[:, 4],
            row_index[:, 5],
            row_index[:, 6],
            row_index[:, 7],
        ],
        1,
    )
    time_back = hop_full[:, 3]

    def operator_apply(vectors):
        return operate(vectors, matrices, pool_index, time_back)

    basis = start_basis
    filtered_block = filtered(basis, operator_apply)
    everything = lax.all_gather(filtered_block, "vec", axis=2, tiled=True).reshape(-1, all_cols)
    own_block = filtered_block.reshape(-1, local_cols)
    gram_part = jnp.einsum("rc,rk->ck", everything, own_block, precision=highest)
    gram_part = lax.psum(gram_part, "site")
    gram_whole = lax.all_gather(gram_part, "vec", axis=1, tiled=True)
    inverse = factor_inverse(gram_whole / total_rows)
    own_rows = lax.dynamic_slice_in_dim(inverse, col_start, local_cols, 0)
    basis_flat = jnp.einsum("rc,kc->rk", everything, own_rows, precision=highest)
    image_block = operator_apply(basis_flat.reshape(filtered_block.shape)).reshape(-1, local_cols)
    moment = jnp.einsum("rc,rk->ck", everything, image_block, precision=highest)
    moment = lax.psum(moment, "site")
    projected = jnp.dot(inverse, moment, precision=highest) / total_rows
    basis = basis_flat.reshape(filtered_block.shape)
    return (basis, projected)


def solution(mesh):
    placed = (
        P("site", None, None),
        P("site", None, None, None),
        P("site", None),
        P("site", None, "vec"),
    )
    return jax.shard_map(
        local,
        mesh=mesh,
        in_specs=placed,
        out_specs=(P("site", None, "vec"), P(None, "vec")),
        check_vma=False,
    )
```

profile of v0, /device:TPU:2, one launch (start us, length us, event | category | flops | bytes accessed | tf_op | source)
XLA Modules:
  0.0 910.2 jit_solution(3755153946303805086)
XLA Ops:
  7.2 14.0 %collective-permute-start = (f32[8,128,64]{1,2,0:T(8,128)}, f32[8,128,64]{1,2,0:T(8,128)}, u32[]{:S(2)}, u32[]{:S(2)}) collective-permute-start(f32[8,128,64]{1,2,0:T(8,128)} %param.13), channel_id=1, source_target_pairs={{0,504},{8,0},{16,8},{24,16},{32,24},{40,32},{48,40},{56,48},{64,5... | collective-permute-start | bytes 786440 | tf_op jit(solution)/shard_map/ppermute | solution.py:14
  30.0 2.4 gather_fusion.1
  33.7 2.4 gather_fusion.2
  36.2 2.0 copy.9
  42.1 2.0 gather_fusion.3
  45.6 7.6 broadcast_multiply_fusion.1
  53.2 7.2 collective-permute-start.2
  61.8 2.1 collective-permute-start.3
  65.5 2.0 gather_fusion.5
  67.5 7.0 collective-permute-done.3
  76.0 7.6 fusion.61
  86.8 3.9 collective-permute-start.5
  92.0 2.0 gather_fusion.7
  94.0 4.7 collective-permute-done.5
  99.2 7.6 fusion.49
  106.8 1.9 collective-permute-start.6
  109.3 3.9 collective-permute-start.7
  115.1 2.0 gather_fusion.9
  117.1 3.9 collective-permute-done.7
  122.6 8.3 fusion.37
  131.0 20.6 %all-gather.3.cloned.1.call-done = f32[8,128,512]{1,2,0:T(8,128)} async-done(((f32[8,128,64]{1,2,0:T(8,128)}), f32[8,128,512]{1,2,0:T(8,128)}) %all-gather.3.cloned.1.call-update) | async-done | bytes 2097168 | tf_op jit(solution)/shard_map/all_gather | solution.py:91
  151.6 4.4 convolution_bitcast_fusion.1
  156.0 262.2 %all-reduce.4.cloned.1.call-done = f32[512,64]{0,1:T(8,128)} async-done(((f32[512,64]{0,1:T(8,128)}), f32[512,64]{0,1:T(8,128)}) %all-reduce.4.cloned.1.call-update) | async-done | bytes 131088 | tf_op jit(solution)/shard_map/psum | solution.py:94
  420.6 23.9 %all-gather.5.cloned.1.call-done = f32[512,512]{0,1:T(8,128)} async-done(((f32[512,64]{0,1:T(8,128)}), f32[512,512]{0,1:T(8,128)}) %all-gather.5.cloned.1.call-update) | async-done | bytes 1048592 | tf_op jit(solution)/shard_map/all_gather | solution.py:95
  444.5 2.4 broadcast_multiply_fusion
  446.9 2.6 copy.10
  452.0 11.7 %cholesky.104 = f32[128,128]{1,0:T(8,128)S(1)} custom-call(f32[128,128]{1,0:T(8,128)S(1)} %cholesky.266), custom_call_target="Cholesky" | custom-call | tf_op jit(solution)/shard_map/jit(cholesky)/cholesky | solution.py:48
  463.9 9.8 %custom-call.31 = f32[1,128,128]{1,2,0:T(8,128)S(1)} custom-call(f32[1,128,128]{2,1,0:T(8,128)S(1)} %get-tuple-element.47), custom_call_target="InvertDiagBlocksLowerTriangular" | custom-call | tf_op jit(solution)/shard_map/jit(cholesky)/cholesky | solution.py:48
  476.2 11.7 %cholesky.217 = f32[128,128]{1,0:T(8,128)S(1)} custom-call(f32[128,128]{1,0:T(8,128)S(1)} %cholesky.270), custom_call_target="Cholesky" | custom-call | tf_op jit(solution)/shard_map/jit(cholesky)/cholesky | solution.py:48
  489.3 9.9 %custom-call.32 = f32[1,128,128]{1,2,0:T(8,128)S(1)} custom-call(f32[1,128,128]{2,1,0:T(8,128)S(1)} %get-tuple-element.44), custom_call_target="InvertDiagBlocksLowerTriangular" | custom-call | tf_op jit(solution)/shard_map/jit(cholesky)/cholesky | solution.py:48
  500.8 11.7 %cholesky.238 = f32[128,128]{1,0:T(8,128)S(1)} custom-call(f32[128,128]{1,0:T(8,128)S(1)} %cholesky.275), custom_call_target="Cholesky" | custom-call | tf_op jit(solution)/shard_map/jit(cholesky)/cholesky | solution.py:48
  513.2 9.8 %custom-call.33 = f32[1,128,128]{1,2,0:T(8,128)S(1)} custom-call(f32[1,128,128]{2,1,0:T(8,128)S(1)} %get-tuple-element.41), custom_call_target="InvertDiagBlocksLowerTriangular" | custom-call | tf_op jit(solution)/shard_map/jit(cholesky)/cholesky | solution.py:48
  524.5 11.9 %cholesky.255 = f32[128,128]{1,0:T(8,128)S(1)} custom-call(f32[128,128]{1,0:T(8,128)S(1)} %convolution_subtract_fusion.5), custom_call_target="Cholesky" | custom-call | tf_op jit(solution)/shard_map/jit(cholesky)/cholesky | solution.py:48
  540.8 14.3 %while.1 = (s32[]{:T(128)}, f32[512,512]{1,0:T(8,128)}, s32[4,2]{0,1:T(2,128)S(1)}, f32[4,128,128]{2,1,0:T(8,128)}, s32[]{:T(128)}) while((s32[]{:T(128)}, f32[512,512]{1,0:T(8,128)}, s32[4,2]{0,1:T(2,128)S(1)}, f32[4,128,128]{2,1,0:T(8,128)}, s32[]{:T(128)}) %tuple.47), condition=%wide.while_cond, body=%wide.while_body.sunk | while | flops 2 | bytes 132705 | solution.py:50
  541.5 2.9 bitcast_dynamic-update-slice_fusion.5
  545.1 2.9 bitcast_dynamic-update-slice_fusion.5
  548.6 2.9 bitcast_dynamic-update-slice_fusion.5
  552.2 2.9 bitcast_dynamic-update-slice_fusion.5
  555.1 40.1 %custom-call.34 = f32[4,128,128]{1,2,0:T(8,128)S(1)} custom-call(f32[4,128,128]{2,1,0:T(8,128)} %get-tuple-element.12), custom_call_target="InvertDiagBlocksLowerTriangular" | custom-call | tf_op jit(solution)/shard_map/jit(_solve_triangular)/triangular_solve | solution.py:50
  604.8 7.7 collective-permute-start.8
  614.3 2.2 collective-permute-start.9
  616.5 2.0 collective-permute-done.8
  618.5 2.0 gather_fusion.11
  620.5 13.0 %collective-permute-done.9 = f32[8,128,64]{2,1,0:T(8,128)S(1)} collective-permute-done((f32[8,128,64]{2,1,0:T(8,128)}, f32[8,128,64]{2,1,0:T(8,128)S(1)}, u32[]{:S(2)}, u32[]{:S(2)}) %collective-permute-start.9) | collective-permute-done | bytes 262176 | tf_op jit(solution)/shard_map/ppermute | solution.py:14
  634.9 6.8 fusion.13
  641.8 2.5 convolution_bitcast_fusion
  644.3 256.3 %all-reduce.6.cloned.1.call-done = f32[512,64]{1,0:T(8,128)} async-done(((f32[512,64]{1,0:T(8,128)}), f32[512,64]{1,0:T(8,128)}) %all-reduce.6.cloned.1.call-update) | async-done | bytes 131088 | tf_op jit(solution)/shard_map/psum | solution.py:101
  900.7 2.7 convolution_multiply_fusion
  (124 shorter events, 58.6 us)
Async XLA Ops:
  7.2 15.2 %copy-start.4 = (f32[8,4,64,128]{3,2,1,0:T(8,128)S(1)}, f32[8,4,64,128]{3,2,1,0:T(8,128)}, u32[]{:S(2)}) copy-start(f32[8,4,64,128]{3,2,1,0:T(8,128)} %param.11) | copy-start | bytes 3145732
  7.2 144.4 %all-gather.3.cloned.1.call-start = ((), (), s32[]{:S(2)}) async-start(), calls=%async_computation | async-start | bytes 2359296 | tf_op jit(solution)/shard_map/all_gather | solution.py:91
  7.2 33.9 %collective-permute-start = (f32[8,128,64]{1,2,0:T(8,128)}, f32[8,128,64]{1,2,0:T(8,128)}, u32[]{:S(2)}, u32[]{:S(2)}) collective-permute-start(f32[8,128,64]{1,2,0:T(8,128)} %param.13), channel_id=1, source_target_pairs={{0,504},{8,0},{16,8},{24,16},{32,24},{40,32},{48,40},{56,48},{64,5... | collective-permute-start | bytes 786440 | tf_op jit(solution)/shard_map/ppermute | solution.py:14
  23.0 1.0 copy-start.5
  23.6 5.1 copy-start
  24.0 4.8 copy-start.10
  25.7 18.3 %collective-permute-start.1 = (f32[8,128,64]{1,2,0:T(8,128)}, f32[8,128,64]{1,2,0:T(8,128)}, u32[]{:S(2)}, u32[]{:S(2)}) collective-permute-start(f32[8,128,64]{1,2,0:T(8,128)} %fusion.94), channel_id=1, source_target_pairs={{0,8},{8,16},{16,24},{24,32},{32,40},{40,48},{48,56},{56,64},{64,7... | collective-permute-start | bytes 786440 | tf_op jit(solution)/shard_map/ppermute | solution.py:14
  38.2 1.9 copy-start.8
  53.2 12.2 %collective-permute-start.2 = (f32[8,128,64]{1,2,0:T(8,128)S(1)}, f32[8,128,64]{1,2,0:T(8,128)S(1)}, u32[]{:S(2)}, u32[]{:S(2)}) collective-permute-start(f32[8,128,64]{1,2,0:T(8,128)S(1)} %get-tuple-element.49), channel_id=1, source_target_pairs={{0,504},{8,0},{16,8},{24,16},{32,24},{40,32},{48,40},{56,48},{64,5... | collective-permute-start | bytes 786440 | tf_op jit(solution)/shard_map/ppermute | solution.py:14
  61.8 12.7 %collective-permute-start.3 = (f32[8,128,64]{1,2,0:T(8,128)}, f32[8,128,64]{1,2,0:T(8,128)}, u32[]{:S(2)}, u32[]{:S(2)}) collective-permute-start(f32[8,128,64]{1,2,0:T(8,128)} %fusion.93), channel_id=1, source_target_pairs={{0,8},{8,16},{16,24},{24,32},{32,40},{40,48},{48,56},{56,64},{64,7... | collective-permute-start | bytes 786440 | tf_op jit(solution)/shard_map/ppermute | solution.py:14
  83.6 8.3 collective-permute-start.4
  86.8 11.8 %collective-permute-start.5 = (f32[8,128,64]{1,2,0:T(8,128)}, f32[8,128,64]{1,2,0:T(8,128)S(1)}, u32[]{:S(2)}, u32[]{:S(2)}) collective-permute-start(f32[8,128,64]{1,2,0:T(8,128)} %fusion.92), channel_id=1, source_target_pairs={{0,8},{8,16},{16,24},{24,32},{32,40},{40,48},{48,56},{56,64},{64,7... | collective-permute-start | bytes 786440 | tf_op jit(solution)/shard_map/ppermute | solution.py:14
  106.8 8.3 collective-permute-start.6
  109.3 11.7 %collective-permute-start.7 = (f32[8,128,64]{1,2,0:T(8,128)S(1)}, f32[8,128,64]{1,2,0:T(8,128)}, u32[]{:S(2)}, u32[]{:S(2)}) collective-permute-start(f32[8,128,64]{1,2,0:T(8,128)S(1)} %fusion.91), channel_id=1, source_target_pairs={{0,8},{8,16},{16,24},{24,32},{32,40},{40,48},{48,56},{56,64},{64,7... | collective-permute-start | bytes 786440 | tf_op jit(solution)/shard_map/ppermute | solution.py:14
  130.9 287.2 %all-reduce.4.cloned.1.call-start = ((), (), s32[]{:S(2)}) async-start(), calls=%async_computation.1 | async-start | bytes 262144 | tf_op jit(solution)/shard_map/psum | solution.py:94
  156.0 288.5 %all-gather.5.cloned.1.call-start = ((), (), s32[]{:S(2)}) async-start(), calls=%async_computation.2 | async-start | bytes 1179648 | tf_op jit(solution)/shard_map/all_gather | solution.py:95
  418.2 482.5 %all-reduce.6.cloned.1.call-start = ((), (), s32[]{:S(2)}) async-start(), calls=%async_computation.3 | async-start | bytes 524288 | tf_op jit(solution)/shard_map/psum | solution.py:101
  444.5 5.0 copy-start.3
  450.9 1.0 copy-start.6
  595.2 4.9 copy-start.9
  600.1 3.2 copy-start.1
  604.8 15.8 %copy-start.7 = (f32[8,128,64]{1,2,0:T(8,128)}, f32[8,128,64]{1,2,0:T(8,128)S(1)}, u32[]{:S(2)}) copy-start(f32[8,128,64]{1,2,0:T(8,128)S(1)} %fusion.106) | copy-start | bytes 786436
  604.8 13.7 %collective-permute-start.8 = (f32[8,128,64]{1,2,0:T(8,128)S(1)}, f32[8,128,64]{1,2,0:T(8,128)S(1)}, u32[]{:S(2)}, u32[]{:S(2)}) collective-permute-start(f32[8,128,64]{1,2,0:T(8,128)S(1)} %fusion.106), channel_id=1, source_target_pairs={{0,504},{8,0},{16,8},{24,16},{32,24},{40,32},{48,40},{56,48},{64,5... | collective-permute-start | bytes 786440 | tf_op jit(solution)/shard_map/ppermute | solution.py:14
  614.3 19.2 %collective-permute-start.9 = (f32[8,128,64]{2,1,0:T(8,128)}, f32[8,128,64]{2,1,0:T(8,128)S(1)}, u32[]{:S(2)}, u32[]{:S(2)}) collective-permute-start(f32[8,128,64]{2,1,0:T(8,128)} %fusion.90), channel_id=1, source_target_pairs={{0,8},{8,16},{16,24},{24,32},{32,40},{40,48},{48,56},{56,64},{64,7... | collective-permute-start | bytes 786440 | tf_op jit(solution)/shard_map/ppermute | solution.py:14
  634.9 6.9 copy-start.2
Sparse Core Ops, SparseCore 0:
  131.0 20.4 all-gather.2
  156.1 262.0 all-reduce.3
  420.3 24.1 all-gather.4
  644.5 256.1 all-reduce.5
where the time goes:
time: 918 us; the launch traced here: 910 us
  waiting for transfers between devices  598 us (65%)
  other arithmetic  133 us (14%)
  matrix products  69.3 us (8%)
  starting transfers between devices  47.3 us (5%)
  local copies, waits for them, and re-layouts  45.1 us (5%)
  between operations  17.2 us (2%)
    psum x1, waiting for transfers between devices, local(): gram_part = lax.psum(gram_part, 'site')  262 us
    psum x1, waiting for transfers between devices, local(): moment = lax.psum(moment, 'site')  256 us
    another operation x15, other arithmetic, factor_inverse(): lower_factor = jnp.linalg.cholesky(gram_matrix)  79.4 us
    ppermute x10, starting transfers between devices, passed_along(): return lax.ppermute(x, axis, [(i, (i + by) % size) for i in range(size)])  46.7 us
    another operation x4, other arithmetic, factor_inverse(): return jax.scipy.linalg.solve_triangular(lower_factor, identity, lower=True)  41.3 us
    dot_general x5, matrix products, operate(): summed = jnp.einsum('sjab,sjbc->sac', matrices, sources, precision=highest)  38.1 us
    ppermute x10, waiting for transfers between devices, passed_along(): return lax.ppermute(x, axis, [(i, (i + by) % size) for i in range(size)])  35.1 us
    all_gather x1, waiting for transfers between devices, local(): gram_whole = lax.all_gather(gram_part, 'vec', axis=1, tiled=True)  23.9 us
  transfers between devices with their start and end apart: 14, of which 12 were waited for; matrix products, arithmetic and copies ran while one was open for 4% of the time, Pallas kernels for 0%

commit v1 on v0

--- a/solution.py
+++ b/solution.py
@@ -7,6 +7,11 @@
 filter_center = 3.7
 filter_radius = 3.1
 highest = lax.Precision.HIGHEST
+
+
+def add_all(array, axis):
+    pieces = lax.all_gather(array, axis)
+    return jnp.sum(pieces, axis=0)
 
 
 def passed_along(x, axis, by):
@@ -91,7 +96,7 @@
     everything = lax.all_gather(filtered_block, "vec", axis=2, tiled=True).reshape(-1, all_cols)
     own_block = filtered_block.reshape(-1, local_cols)
     gram_part = jnp.einsum("rc,rk->ck", everything, own_block, precision=highest)
-    gram_part = lax.psum(gram_part, "site")
+    gram_part = add_all(gram_part, "site")
     gram_whole = lax.all_gather(gram_part, "vec", axis=1, tiled=True)
     inverse = factor_inverse(gram_whole / total_rows)
     own_rows = lax.dynamic_slice_in_dim(inverse, col_start, local_cols, 0)

time: 918 us -> 824 us (0.90)
  waiting for transfers between devices: 598 us -> 493 us
    psum x1 -> x0, waiting for transfers between devices: 262 us -> none  [local(): gram_part = lax.psum(gram_part, 'site')]
    all_gather x0 -> x1, waiting for transfers between devices: none -> 159 us  [add_all(): pieces = lax.all_gather(array, axis)]
where the time goes in v1:
time: 824 us; the launch traced here: 817 us
  waiting for transfers between devices  493 us (60%)
  other arithmetic  136 us (17%)
  matrix products  69.2 us (8%)
  local copies, waits for them, and re-layouts  53.4 us (6%)
  starting transfers between devices  47.8 us (6%)
  between operations  17.3 us (2%)
    psum x1, waiting for transfers between devices, local(): moment = lax.psum(moment, 'site')  257 us
    all_gather x1, waiting for transfers between devices, add_all(): pieces = lax.all_gather(array, axis)  159 us
    another operation x15, other arithmetic, factor_inverse(): lower_factor = jnp.linalg.cholesky(gram_matrix)  79.4 us
    ppermute x10, starting transfers between devices, passed_along(): return lax.ppermute(x, axis, [(i, (i + by) % size) for i in range(size)])  47.2 us
    another operation x4, other arithmetic, factor_inverse(): return jax.scipy.linalg.solve_triangular(lower_factor, identity, lower=True)  41.4 us
    dot_general x5, matrix products, operate(): summed = jnp.einsum('sjab,sjbc->sac', matrices, sources, precision=highest)  38.1 us
    ppermute x10, waiting for transfers between devices, passed_along(): return lax.ppermute(x, axis, [(i, (i + by) % size) for i in range(size)])  34.5 us
    all_gather x1, waiting for transfers between devices, local(): gram_whole = lax.all_gather(gram_part, 'vec', axis=1, tiled=True)  22.4 us
  transfers between devices with their start and end apart: 14, of which 12 were waited for; matrix products, arithmetic and copies ran while one was open for 4% of the time, Pallas kernels for 0%

profile of v1, /device:TPU:2, one launch (start us, length us, event | category | flops | bytes accessed | tf_op | source)
XLA Modules:
  0.0 816.8 jit_solution(16095290115614211450)
XLA Ops:
  7.2 14.0 %collective-permute-start = (f32[8,128,64]{1,2,0:T(8,128)}, f32[8,128,64]{1,2,0:T(8,128)}, u32[]{:S(2)}, u32[]{:S(2)}) collective-permute-start(f32[8,128,64]{1,2,0:T(8,128)} %param.13), channel_id=1, source_target_pairs={{0,504},{8,0},{16,8},{24,16},{32,24},{40,32},{48,40},{56,48},{64,5... | collective-permute-start | bytes 786440 | tf_op jit(solution)/shard_map/ppermute | solution.py:19
  30.0 2.4 gather_fusion.1
  33.7 2.4 gather_fusion.2
  36.1 2.0 copy.9
  42.1 2.0 gather_fusion.3
  45.6 7.6 broadcast_multiply_fusion.1
  53.3 7.2 collective-permute-start.2
  61.8 2.4 collective-permute-start.3
  65.5 2.0 gather_fusion.5
  67.6 7.0 collective-permute-done.3
  76.0 7.6 fusion.61
  86.9 3.9 collective-permute-start.5
  92.0 2.0 gather_fusion.7
  94.0 4.6 collective-permute-done.5
  99.2 7.6 fusion.49
  109.4 4.1 collective-permute-start.7
  115.2 2.0 gather_fusion.9
  117.2 3.9 collective-permute-done.7
  122.6 8.3 %fusion.37 = f32[8,128,64]{1,2,0:T(8,128)} fusion(f32[8,128,64]{1,2,0:T(8,128)S(1)} %fusion.61, f32[8,8,128,128]{3,2,1,0:T(8,128)} %bitcast_dynamic-update-slice_fusion.1, f32[8,8,128,64]{2,3,1,0:T(8,128)} %bitcast.157, pred[8,8]{1,0:T(8,128)(4,1)S(1)} %compare_and_fusion, f32[8,128,64]{1,2,0:T(8,128)S(1)} %gather_fusion.10, f32[8,128,64]{1,2,0:T(8,128)S(1)} %fusion.49, ...), kind=kOutput, calls=%fused_computation.41 | convolution fusion | flops 806223872 | bytes 7340104 | tf_op jit(solution)/shard_map/sjab,sjbc->sac/dot_general | solution.py:35
  131.0 20.6 %all-gather.5.cloned.1.call-done = f32[8,128,512]{1,2,0:T(8,128)} async-done(((f32[8,128,64]{1,2,0:T(8,128)}), f32[8,128,512]{1,2,0:T(8,128)}) %all-gather.5.cloned.1.call-update) | async-done | bytes 2097168 | tf_op jit(solution)/shard_map/all_gather | solution.py:96
  151.6 4.4 convolution_bitcast_fusion.1
  156.0 158.8 %all-gather.9.cloned.1.call-done = f32[32768,64]{0,1:T(8,128)} async-done(((f32[512,64]{0,1:T(8,128)}), f32[32768,64]{0,1:T(8,128)}) %all-gather.9.cloned.1.call-update) | async-done | bytes 8388624 | tf_op jit(solution)/shard_map/all_gather | solution.py:13
  314.8 8.1 copy.16
  323.0 3.1 bitcast_reduce_fusion
  328.4 22.4 %all-gather.7.cloned.1.call-done = f32[512,512]{0,1:T(8,128)} async-done(((f32[512,64]{0,1:T(8,128)}), f32[512,512]{0,1:T(8,128)}) %all-gather.7.cloned.1.call-update) | async-done | bytes 1048592 | tf_op jit(solution)/shard_map/all_gather | solution.py:100
  350.8 2.4 broadcast_multiply_fusion
  353.2 2.6 copy.10
  358.2 11.7 %cholesky.104 = f32[128,128]{1,0:T(8,128)S(1)} custom-call(f32[128,128]{1,0:T(8,128)S(1)} %cholesky.266), custom_call_target="Cholesky" | custom-call | tf_op jit(solution)/shard_map/jit(cholesky)/cholesky | solution.py:53
  370.1 9.8 %custom-call.31 = f32[1,128,128]{1,2,0:T(8,128)S(1)} custom-call(f32[1,128,128]{2,1,0:T(8,128)S(1)} %get-tuple-element.47), custom_call_target="InvertDiagBlocksLowerTriangular" | custom-call | tf_op jit(solution)/shard_map/jit(cholesky)/cholesky | solution.py:53
  382.4 11.7 %cholesky.217 = f32[128,128]{1,0:T(8,128)S(1)} custom-call(f32[128,128]{1,0:T(8,128)S(1)} %cholesky.270), custom_call_target="Cholesky" | custom-call | tf_op jit(solution)/shard_map/jit(cholesky)/cholesky | solution.py:53
  395.5 9.9 %custom-call.32 = f32[1,128,128]{1,2,0:T(8,128)S(1)} custom-call(f32[1,128,128]{2,1,0:T(8,128)S(1)} %get-tuple-element.44), custom_call_target="InvertDiagBlocksLowerTriangular" | custom-call | tf_op jit(solution)/shard_map/jit(cholesky)/cholesky | solution.py:53
  407.0 11.7 %cholesky.238 = f32[128,128]{1,0:T(8,128)S(1)} custom-call(f32[128,128]{1,0:T(8,128)S(1)} %cholesky.275), custom_call_target="Cholesky" | custom-call | tf_op jit(solution)/shard_map/jit(cholesky)/cholesky | solution.py:53
  419.5 9.8 %custom-call.33 = f32[1,128,128]{1,2,0:T(8,128)S(1)} custom-call(f32[1,128,128]{2,1,0:T(8,128)S(1)} %get-tuple-element.41), custom_call_target="InvertDiagBlocksLowerTriangular" | custom-call | tf_op jit(solution)/shard_map/jit(cholesky)/cholesky | solution.py:53
  430.7 11.9 %cholesky.255 = f32[128,128]{1,0:T(8,128)S(1)} custom-call(f32[128,128]{1,0:T(8,128)S(1)} %convolution_subtract_fusion.5), custom_call_target="Cholesky" | custom-call | tf_op jit(solution)/shard_map/jit(cholesky)/cholesky | solution.py:53
  447.2 14.4 %while.1 = (s32[]{:T(128)}, f32[512,512]{1,0:T(8,128)}, s32[4,2]{0,1:T(2,128)S(1)}, f32[4,128,128]{2,1,0:T(8,128)}, s32[]{:T(128)}) while((s32[]{:T(128)}, f32[512,512]{1,0:T(8,128)}, s32[4,2]{0,1:T(2,128)S(1)}, f32[4,128,128]{2,1,0:T(8,128)}, s32[]{:T(128)}) %tuple.47), condition=%wide.while_cond, body=%wide.while_body.sunk | while | flops 2 | bytes 132705 | solution.py:55
  447.8 3.0 bitcast_dynamic-update-slice_fusion.5
  451.4 3.0 bitcast_dynamic-update-slice_fusion.5
  455.0 3.0 bitcast_dynamic-update-slice_fusion.5
  458.6 2.9 bitcast_dynamic-update-slice_fusion.5
  461.5 40.1 %custom-call.34 = f32[4,128,128]{1,2,0:T(8,128)S(1)} custom-call(f32[4,128,128]{2,1,0:T(8,128)} %get-tuple-element.12), custom_call_target="InvertDiagBlocksLowerTriangular" | custom-call | tf_op jit(solution)/shard_map/jit(_solve_triangular)/triangular_solve | solution.py:55
  511.2 7.7 collective-permute-start.8
  520.7 2.2 collective-permute-start.9
  524.9 2.0 gather_fusion.11
  527.0 13.0 %collective-permute-done.9 = f32[8,128,64]{2,1,0:T(8,128)S(1)} collective-permute-done((f32[8,128,64]{2,1,0:T(8,128)}, f32[8,128,64]{2,1,0:T(8,128)S(1)}, u32[]{:S(2)}, u32[]{:S(2)}) %collective-permute-start.9) | collective-permute-done | bytes 262176 | tf_op jit(solution)/shard_map/ppermute | solution.py:19
  541.3 6.8 fusion.13
  548.2 2.5 convolution_bitcast_fusion
  550.7 256.5 %all-reduce.3.cloned.1.call-done = f32[512,64]{1,0:T(8,128)} async-done(((f32[512,64]{1,0:T(8,128)}), f32[512,64]{1,0:T(8,128)}) %all-reduce.3.cloned.1.call-update) | async-done | bytes 131088 | tf_op jit(solution)/shard_map/psum | solution.py:106
  807.2 2.7 convolution_multiply_fusion
  (126 shorter events, 62.0 us)
Async XLA Ops:
  7.2 15.2 %copy-start.4 = (f32[8,4,64,128]{3,2,1,0:T(8,128)S(1)}, f32[8,4,64,128]{3,2,1,0:T(8,128)}, u32[]{:S(2)}) copy-start(f32[8,4,64,128]{3,2,1,0:T(8,128)} %param.11) | copy-start | bytes 3145732
  7.2 144.4 %all-gather.5.cloned.1.call-start = ((), (), s32[]{:S(2)}) async-start(), calls=%async_computation | async-start | bytes 2359296 | tf_op jit(solution)/shard_map/all_gather | solution.py:96
  7.2 33.8 %collective-permute-start = (f32[8,128,64]{1,2,0:T(8,128)}, f32[8,128,64]{1,2,0:T(8,128)}, u32[]{:S(2)}, u32[]{:S(2)}) collective-permute-start(f32[8,128,64]{1,2,0:T(8,128)} %param.13), channel_id=1, source_target_pairs={{0,504},{8,0},{16,8},{24,16},{32,24},{40,32},{48,40},{56,48},{64,5... | collective-permute-start | bytes 786440 | tf_op jit(solution)/shard_map/ppermute | solution.py:19
  23.0 1.0 copy-start.5
  23.6 5.1 copy-start
  24.0 4.8 copy-start.10
  25.7 18.4 %collective-permute-start.1 = (f32[8,128,64]{1,2,0:T(8,128)}, f32[8,128,64]{1,2,0:T(8,128)}, u32[]{:S(2)}, u32[]{:S(2)}) collective-permute-start(f32[8,128,64]{1,2,0:T(8,128)} %fusion.94), channel_id=1, source_target_pairs={{0,8},{8,16},{16,24},{24,32},{32,40},{40,48},{48,56},{56,64},{64,7... | collective-permute-start | bytes 786440 | tf_op jit(solution)/shard_map/ppermute | solution.py:19
  38.2 1.9 copy-start.8
  53.3 12.2 %collective-permute-start.2 = (f32[8,128,64]{1,2,0:T(8,128)S(1)}, f32[8,128,64]{1,2,0:T(8,128)S(1)}, u32[]{:S(2)}, u32[]{:S(2)}) collective-permute-start(f32[8,128,64]{1,2,0:T(8,128)S(1)} %get-tuple-element.49), channel_id=1, source_target_pairs={{0,504},{8,0},{16,8},{24,16},{32,24},{40,32},{48,40},{56,48},{64,5... | collective-permute-start | bytes 786440 | tf_op jit(solution)/shard_map/ppermute | solution.py:19
  61.8 12.7 %collective-permute-start.3 = (f32[8,128,64]{1,2,0:T(8,128)}, f32[8,128,64]{1,2,0:T(8,128)}, u32[]{:S(2)}, u32[]{:S(2)}) collective-permute-start(f32[8,128,64]{1,2,0:T(8,128)} %fusion.93), channel_id=1, source_target_pairs={{0,8},{8,16},{16,24},{24,32},{32,40},{40,48},{48,56},{56,64},{64,7... | collective-permute-start | bytes 786440 | tf_op jit(solution)/shard_map/ppermute | solution.py:19
  83.7 8.3 %collective-permute-start.4 = (f32[8,128,64]{1,2,0:T(8,128)S(1)}, f32[8,128,64]{1,2,0:T(8,128)S(1)}, u32[]{:S(2)}, u32[]{:S(2)}) collective-permute-start(f32[8,128,64]{1,2,0:T(8,128)S(1)} %fusion.61), channel_id=1, source_target_pairs={{0,504},{8,0},{16,8},{24,16},{32,24},{40,32},{48,40},{56,48},{64,5... | collective-permute-start | bytes 786440 | tf_op jit(solution)/shard_map/ppermute | solution.py:19
  86.9 11.8 %collective-permute-start.5 = (f32[8,128,64]{1,2,0:T(8,128)}, f32[8,128,64]{1,2,0:T(8,128)S(1)}, u32[]{:S(2)}, u32[]{:S(2)}) collective-permute-start(f32[8,128,64]{1,2,0:T(8,128)} %fusion.92), channel_id=1, source_target_pairs={{0,8},{8,16},{16,24},{24,32},{32,40},{40,48},{48,56},{56,64},{64,7... | collective-permute-start | bytes 786440 | tf_op jit(solution)/shard_map/ppermute | solution.py:19
  106.9 8.3 %collective-permute-start.6 = (f32[8,128,64]{1,2,0:T(8,128)S(1)}, f32[8,128,64]{1,2,0:T(8,128)S(1)}, u32[]{:S(2)}, u32[]{:S(2)}) collective-permute-start(f32[8,128,64]{1,2,0:T(8,128)S(1)} %fusion.49), channel_id=1, source_target_pairs={{0,504},{8,0},{16,8},{24,16},{32,24},{40,32},{48,40},{56,48},{64,5... | collective-permute-start | bytes 786440 | tf_op jit(solution)/shard_map/ppermute | solution.py:19
  109.4 11.7 %collective-permute-start.7 = (f32[8,128,64]{1,2,0:T(8,128)S(1)}, f32[8,128,64]{1,2,0:T(8,128)}, u32[]{:S(2)}, u32[]{:S(2)}) collective-permute-start(f32[8,128,64]{1,2,0:T(8,128)S(1)} %fusion.91), channel_id=1, source_target_pairs={{0,8},{8,16},{16,24},{24,32},{32,40},{40,48},{48,56},{56,64},{64,7... | collective-permute-start | bytes 786440 | tf_op jit(solution)/shard_map/ppermute | solution.py:19
  131.0 183.9 %all-gather.9.cloned.1.call-start = ((), (), s32[]{:S(2)}) async-start(), calls=%async_computation.3 | async-start | bytes 8519680 | tf_op jit(solution)/shard_map/all_gather | solution.py:13
  156.0 194.8 %all-gather.7.cloned.1.call-start = ((), (), s32[]{:S(2)}) async-start(), calls=%async_computation.1 | async-start | bytes 1179648 | tf_op jit(solution)/shard_map/all_gather | solution.py:100
  326.0 481.2 %all-reduce.3.cloned.1.call-start = ((), (), s32[]{:S(2)}) async-start(), calls=%async_computation.2 | async-start | bytes 524288 | tf_op jit(solution)/shard_map/psum | solution.py:106
  350.8 5.0 copy-start.3
  357.2 1.0 copy-start.6
  501.7 4.9 copy-start.9
  506.5 3.2 copy-start.1
  511.2 15.8 %copy-start.7 = (f32[8,128,64]{1,2,0:T(8,128)}, f32[8,128,64]{1,2,0:T(8,128)S(1)}, u32[]{:S(2)}) copy-start(f32[8,128,64]{1,2,0:T(8,128)S(1)} %fusion.106) | copy-start | bytes 786436
  511.2 13.7 %collective-permute-start.8 = (f32[8,128,64]{1,2,0:T(8,128)S(1)}, f32[8,128,64]{1,2,0:T(8,128)S(1)}, u32[]{:S(2)}, u32[]{:S(2)}) collective-permute-start(f32[8,128,64]{1,2,0:T(8,128)S(1)} %fusion.106), channel_id=1, source_target_pairs={{0,504},{8,0},{16,8},{24,16},{32,24},{40,32},{48,40},{56,48},{64,5... | collective-permute-start | bytes 786440 | tf_op jit(solution)/shard_map/ppermute | solution.py:19
  520.7 19.2 %collective-permute-start.9 = (f32[8,128,64]{2,1,0:T(8,128)}, f32[8,128,64]{2,1,0:T(8,128)S(1)}, u32[]{:S(2)}, u32[]{:S(2)}) collective-permute-start(f32[8,128,64]{2,1,0:T(8,128)} %fusion.90), channel_id=1, source_target_pairs={{0,8},{8,16},{16,24},{24,32},{32,40},{40,48},{48,56},{56,64},{64,7... | collective-permute-start | bytes 786440 | tf_op jit(solution)/shard_map/ppermute | solution.py:19
  541.3 6.9 copy-start.2
Sparse Core Ops, SparseCore 0:
  131.1 20.4 all-gather.4
  156.1 158.6 all-gather.8
  326.2 24.5 all-gather.6
  550.8 256.3 all-reduce.2
